TPU v7x, 32 devices: a whole 2x2x4 slice. The times are simulated.
32 devices in a mesh: dp: 2 (over x), seq: 8 (over z, core), tensor: 2 (over y).
Axes of the slice: x: 2, y: 2, z: 4, core: 2. Of those that a mesh axis runs over, the one named last changes fastest.
Arguments:
- events: bfloat16 [4, 2048, 1536], P('dp', 'seq', 'tensor'), may hold values from -6 to 6
- gate_in: bfloat16 [4, 2048, 1536], P('dp', 'seq', 'tensor'), may hold values from -6 to 6
- filters: bfloat16 [1024, 1536], P(None, 'tensor'), may hold values from -0.1875 to 0.1875
- proj: bfloat16 [1536, 1536], P('tensor'), may hold values from -0.15625 to 0.15625
- lengths: int32 [4], P('dp'), may hold values from 256 to 2048, as said below
- cotangent: bfloat16 [4, 2048, 1536], P('dp', 'seq', 'tensor'), may hold values from -6 to 6
Outputs:
- mixed: bfloat16 [4, 2048, 1536], P('dp', 'seq', 'tensor')
- grad_input: bfloat16 [4, 2048, 1536], P('dp', 'seq', 'tensor')
- grad_gate: bfloat16 [4, 2048, 1536], P('dp', 'seq', 'tensor')
- grad_filters: float32 [1024, 1536], P(None, 'tensor')
- grad_proj: float32 [1536, 1536], P('tensor')
Inputs may be any that keep to these rules, and one draw needn't show every extreme that they name: `lengths`: each length is a multiple of 256, and some user's length is 2048.
All inputs are finite; a program needn't handle non-finite values.
Results may differ from a plain program's by a relative error of at most 0.0049.
Values may be sent and summed in bfloat16 or wider, within the bound.
No kernel may reach another device: no remote copies, remote signals or barrier semaphores. Data moves between devices by JAX's collectives and lax.ppermute only.
A program may use at most 128 MiB of HBM per device.

v0:
```python
import math
import jax
import jax.numpy as jnp
from jax import lax
from jax.sharding import PartitionSpec as P


def shifted(value, axis, by):
    count = lax.axis_size(axis)
    pairs = [(i, i + by) for i in range(count) if 0 <= i + by < count]
    return lax.ppermute(value, axis, pairs)


def depthwise(lhs, kernel):
    return lax.conv_general_dilated(
        lhs,
        kernel[:, None, :],
        (1,),
        "VALID",
        dimension_numbers=("NWC", "WIO", "NWC"),
        feature_group_count=lhs.shape[2],
        preferred_element_type=jnp.float32,
    )


def filter_grad(window, grad_conv):
    users, width, chans = window.shape
    length = grad_conv.shape[1]
    lhs = jnp.transpose(window, (1, 0, 2)).reshape(1, width, users * chans)
    kernel = jnp.transpose(grad_conv, (1, 0, 2)).reshape(length, users * chans)
    result = depthwise(lhs, kernel)
    return jnp.sum(result.reshape(-1, users, chans), axis=1)[::-1]


def shards(events, gate_in, filters, proj, lengths, cotangent):
    users, block_len, chans = events.shape
    taps_len = filters.shape[0]
    reach = taps_len // block_len
    first = lax.axis_index("seq") * block_len
    position = first + jnp.arange(block_len, dtype=jnp.int32)
    live = (position[None, :] < lengths[:, None]).astype(jnp.float32)[:, :, None]
    masked = (events.astype(jnp.float32) * live).astype(jnp.bfloat16)
    earlier = []
    for offset in range(1, reach + 1):
        earlier.append(shifted(masked, "seq", offset))
    window = jnp.concatenate(earlier[::-1] + [masked], axis=1)[:, 1:]
    conv = depthwise(window, filters[::-1])
    gate_f = gate_in.astype(jnp.float32)
    gate_sig = jax.nn.sigmoid(gate_f)
    silu_g = gate_f * gate_sig
    gated = (silu_g * conv * live).astype(jnp.bfloat16)
    gated_rows = gated.reshape(-1, chans)
    partial_out = jnp.dot(gated_rows, proj, preferred_element_type=jnp.float32)
    out_rows = lax.psum_scatter(partial_out, "tensor", scatter_dimension=1, tiled=True)
    mixed = out_rows.astype(jnp.bfloat16).reshape(users, block_len, chans)
    cot_rows = cotangent.reshape(-1, chans)
    piece = lax.all_gather(cot_rows, "tensor", axis=1, tiled=True)
    grad_acc = lax.dot_general(
        piece, proj, (((1,), (1,)), ((), ())), preferred_element_type=jnp.float32
    )
    outer = lax.dot_general(
        gated_rows, piece, (((0,), (0,)), ((), ())), preferred_element_type=jnp.float32
    )
    grad_gated = grad_acc.reshape(users, block_len, chans) * live
    grad_conv = (grad_gated * silu_g).astype(jnp.bfloat16)
    grad_gate = (grad_gated * conv * gate_sig * (1.0 + gate_f * (1.0 - gate_sig))).astype(
        jnp.bfloat16
    )
    following = [grad_conv]
    for offset in range(1, reach + 1):
        following.append(shifted(grad_conv, "seq", -offset))
    ahead = jnp.concatenate(following, axis=1)[:, : block_len + taps_len - 1]
    grad_input = (depthwise(ahead, filters) * live).astype(jnp.bfloat16)
    filter_local = filter_grad(window, grad_conv)
    filter_sum, proj_sum = lax.psum((filter_local, outer), ("dp", "seq"))
    scale = 1.0 / math.sqrt(users * lax.axis_size("dp") * block_len * lax.axis_size("seq"))
    return (mixed, grad_input, grad_gate, filter_sum * scale, proj_sum * scale)


def solution(mesh):
    in_specs = (
        P("dp", "seq", "tensor"),
        P("dp", "seq", "tensor"),
        P(None, "tensor"),
        P("tensor", None),
        P("dp"),
        P("dp", "seq", "tensor"),
    )
    out_specs = (
        P("dp", "seq", "tensor"),
        P("dp", "seq", "tensor"),
        P("dp", "seq", "tensor"),
        P(None, "tensor"),
        P("tensor", None),
    )
    return jax.shard_map(shards, mesh=mesh, in_specs=in_specs, out_specs=out_specs, check_vma=False)
```

profile of v0, /device:TPU:0, one launch (start us, length us, event | category | flops | bytes accessed | tf_op | source)
XLA Modules:
  0.0 1037.7 jit_solution(3310441541021366550)
XLA Ops:
  9.5 6.9 collective-permute-start
  16.3 3.6 collective-permute-start.1
  19.9 3.0 collective-permute-start.2
  25.1 23.0 %rev.6 = bf16[1024,768]{1,0:T(8,128)(2,1)} reverse(bf16[1024,768]{1,0:T(8,128)(2,1)} %param.8), dimensions={0} | reverse | bytes 3145728 | tf_op jit(solution)/shard_map/rev | solution.py:47
  51.4 15.7 %collective-permute-done.2 = bf16[2,256,768]{2,1,0:T(8,128)(2,1)} collective-permute-done((bf16[2,256,768]{2,1,0:T(8,128)(2,1)S(1)}, bf16[2,256,768]{2,1,0:T(8,128)(2,1)}, u32[]{:S(2)}, u32[]{:S(2)}) %collective-permute-start.2) | collective-permute-done | bytes 786464 | tf_op jit(solution)/shard_map/ppermute | solution.py:11
  69.7 224.4 %fusion.2 = f32[2,256,768]{2,0,1:T(2,128)} fusion(bf16[2,1280,768]{2,1,0:T(8,128)(2,1)S(1)} %constant_dynamic-update-slice_fusion, bf16[1024,1,768]{2,0,1:T(8,128)(2,1)S(1)} %bitcast.26), kind=kOutput, calls=%fused_computation.3 | convolution fusion | flops 805306368 | bytes 7077888 | tf_op jit(solution)/shard_map/conv_general_dilated | solution.py:15
  294.1 3.0 slice_bitcast_fusion
  297.1 6.3 copy.43
  303.3 16.7 %copy.45 = bf16[1,1279,1536]{2,0,1:T(2,128)(2,1)} copy(bf16[1,1279,1536]{1,2,0:T(8,128)(2,1)} %bitcast.19) | data formatting | bytes 7858176 | tf_op jit(solution)/shard_map/reshape | solution.py:29
  320.0 2.9 fusion.14
  332.3 2.9 copy.46
  335.3 193.4 %convolution_reduce_fusion = f32[1024,1536]{1,0:T(8,128)} fusion(bf16[1,1279,1536]{2,0,1:T(2,128)(2,1)} %copy.45, bf16[256,1,1536]{2,1,0:T(2,128)(2,1)} %copy.46), kind=kOutput, calls=%fused_computation.23 | convolution fusion | flops 805306368 | bytes 11006976 | tf_op jit(solution)/shard_map/conv_general_dilated | solution.py:15
  528.7 8.3 reshape.66
  536.9 11.9 %reduce_sum.9 = f32[1024,768]{1,0:T(8,128)} reduce(f32[1024,2,768]{2,1,0:T(2,128)} %reshape.66, f32[]{:T(128)} %constant.19.clone.1), dimensions={1}, to_apply=%region_1.0 | reduce | flops 786432 | bytes 9437188 | tf_op jit(solution)/shard_map/reduce_sum | solution.py:32
  548.9 24.7 %rev.7 = f32[1024,768]{1,0:T(8,128)} reverse(f32[1024,768]{1,0:T(8,128)} %reduce_sum.9), dimensions={0} | reverse | bytes 6291456 | tf_op jit(solution)/shard_map/rev | solution.py:32
  575.6 2.2 constant_dynamic-update-slice_fusion.7
  582.0 195.2 %fusion = f32[2,256,768]{2,0,1:T(2,128)S(1)} fusion(bf16[2,1280,768]{2,1,0:T(8,128)(2,1)} %constant_dynamic-update-slice_fusion.5, bf16[1024,1,768]{2,0,1:T(8,128)(2,1)S(1)} %bitcast.25), kind=kOutput, calls=%fused_computation.1 | convolution fusion | flops 805306368 | bytes 7077888 | tf_op jit(solution)/shard_map/conv_general_dilated | solution.py:15
  779.3 3.6 fusion.15
  783.0 3.1 fusion.13
  786.2 196.6 %all-reduce.3.cloned.1.call-done = (f32[1024,768]{1,0:T(8,128)}, f32[768,1536]{1,0:T(8,128)}) async-done(((f32[1024,768]{1,0:T(8,128)}, f32[768,1536]{1,0:T(8,128)}), (f32[1024,768]{1,0:T(8,128)}, f32[768,1536]{1,0:T(8,128)})) %all-reduce.3.cloned.1.call-update) | async-done | bytes 7864336 | tf_op jit(solution)/shard_map/psum | solution.py:75
  982.8 4.0 broadcast_multiply_fusion.1
  986.8 2.7 broadcast_multiply_fusion
  989.5 39.1 %reduce-scatter.2.cloned.1.call-done = f32[512,768]{1,0:T(8,128)} async-done(((f32[512,1536]{1,0:T(8,128)}), f32[512,768]{1,0:T(8,128)}) %reduce-scatter.2.cloned.1.call-update) | async-done | bytes 1572880 | tf_op jit(solution)/shard_map/reduce_scatter | solution.py:54
  1028.6 2.4 convert_element_type.36
  (61 shorter events, 28.1 us)
Async XLA Ops:
  7.2 312.9 %copy-start = (bf16[768,1536]{1,0:T(8,128)(2,1)S(1)}, bf16[768,1536]{1,0:T(8,128)(2,1)}, u32[]{:S(2)}) copy-start(bf16[768,1536]{1,0:T(8,128)(2,1)} %param.9) | copy-start | bytes 7077892
  7.2 312.8 %all-gather.2.cloned.1.call-start = ((), (), s32[]{:S(2)}) async-start(), calls=%async_computation.2 | async-start | bytes 2359296 | tf_op jit(solution)/shard_map/all_gather | solution.py:57
  8.1 61.4 %copy-start.11 = (f32[2,256]{1,0:T(2,128)}, f32[2,256]{1,0:T(2,128)S(1)}, u32[]{:S(2)}) copy-start(f32[2,256]{1,0:T(2,128)S(1)} %compare_convert_fusion) | copy-start | bytes 6148
  9.5 38.7 %collective-permute-start = (bf16[2,256,768]{2,1,0:T(8,128)(2,1)S(1)}, bf16[2,256,768]{2,1,0:T(8,128)(2,1)}, u32[]{:S(2)}, u32[]{:S(2)}) collective-permute-start(bf16[2,256,768]{2,1,0:T(8,128)(2,1)S(1)} %multiply_convert_fusion.2), channel_id=1, source_target_pairs={{0,8},{2,10},{4,12},{6,14},{1,9},{3,11},{5,13},{7,15},{16,24},{18,... | collective-permute-start | bytes 2359304 | tf_op jit(solution)/shard_map/ppermute | solution.py:11
  16.3 33.9 %collective-permute-start.1 = (bf16[2,256,768]{2,1,0:T(8,128)(2,1)S(1)}, bf16[2,256,768]{2,1,0:T(8,128)(2,1)}, u32[]{:S(2)}, u32[]{:S(2)}) collective-permute-start(bf16[2,256,768]{2,1,0:T(8,128)(2,1)S(1)} %multiply_convert_fusion.2), channel_id=1, source_target_pairs={{0,6},{2,8},{4,10},{6,12},{8,14},{1,7},{3,9},{5,11},{7,13},{9,15},... | collective-permute-start | bytes 2359304 | tf_op jit(solution)/shard_map/ppermute | solution.py:11
  19.9 47.2 %collective-permute-start.2 = (bf16[2,256,768]{2,1,0:T(8,128)(2,1)S(1)}, bf16[2,256,768]{2,1,0:T(8,128)(2,1)}, u32[]{:S(2)}, u32[]{:S(2)}) collective-permute-start(bf16[2,256,768]{2,1,0:T(8,128)(2,1)S(1)} %multiply_convert_fusion.2), channel_id=1, source_target_pairs={{0,4},{2,6},{4,8},{6,10},{8,12},{10,14},{1,5},{3,7},{5,9},{7,11},{... | collective-permute-start | bytes 2359304 | tf_op jit(solution)/shard_map/ppermute | solution.py:11
  22.9 45.4 %collective-permute-start.3 = (bf16[2,256,768]{2,1,0:T(8,128)(2,1)S(1)}, bf16[2,256,768]{2,1,0:T(8,128)(2,1)}, u32[]{:S(2)}, u32[]{:S(2)}) collective-permute-start(bf16[2,256,768]{2,1,0:T(8,128)(2,1)S(1)} %multiply_convert_fusion.2), channel_id=1, source_target_pairs={{0,2},{2,4},{4,6},{6,8},{8,10},{10,12},{12,14},{1,3},{3,5},{5,7},{... | collective-permute-start | bytes 2359304 | tf_op jit(solution)/shard_map/ppermute | solution.py:11
  25.1 957.7 %all-reduce.3.cloned.1.call-start = ((), (), s32[]{:S(2)}) async-start(), calls=%async_computation.3 | async-start | bytes 15728640 | tf_op jit(solution)/shard_map/psum | solution.py:75
  49.3 20.1 %copy-start.6 = (bf16[2,256,768]{2,1,0:T(8,128)(2,1)S(1)}, bf16[2,256,768]{2,1,0:T(8,128)(2,1)}, u32[]{:S(2)}) copy-start(bf16[2,256,768]{2,1,0:T(8,128)(2,1)} %param.6) | copy-start | bytes 2359300
  51.4 18.3 %copy-start.9 = (bf16[1024,768]{1,0:T(8,128)(2,1)S(1)}, bf16[1024,768]{1,0:T(8,128)(2,1)}, u32[]{:S(2)}) copy-start(bf16[1024,768]{1,0:T(8,128)(2,1)} %rev.6) | copy-start | bytes 4718596
  320.0 4.1 copy-start.4
  320.0 4.1 copy-start.12
  325.7 247.8 %collective-permute-start.4 = (bf16[2,256,768]{2,1,0:T(8,128)(2,1)}, bf16[2,256,768]{2,1,0:T(8,128)(2,1)}, u32[]{:S(2)}, u32[]{:S(2)}) collective-permute-start(bf16[2,256,768]{2,1,0:T(8,128)(2,1)} %get-tuple-element.18), channel_id=1, source_target_pairs={{2,0},{4,2},{6,4},{8,6},{10,8},{12,10},{14,12},{3,1},{5,3},{7,5},{... | collective-permute-start | bytes 2359304 | tf_op jit(solution)/shard_map/ppermute | solution.py:11
  327.0 248.6 %collective-permute-start.5 = (bf16[2,256,768]{2,1,0:T(8,128)(2,1)}, bf16[2,256,768]{2,1,0:T(8,128)(2,1)}, u32[]{:S(2)}, u32[]{:S(2)}) collective-permute-start(bf16[2,256,768]{2,1,0:T(8,128)(2,1)} %get-tuple-element.18), channel_id=1, source_target_pairs={{4,0},{6,2},{8,4},{10,6},{12,8},{14,10},{5,1},{7,3},{9,5},{11,7},{... | collective-permute-start | bytes 2359304 | tf_op jit(solution)/shard_map/ppermute | solution.py:11
  328.3 249.5 %collective-permute-start.6 = (bf16[2,256,768]{2,1,0:T(8,128)(2,1)}, bf16[2,256,768]{2,1,0:T(8,128)(2,1)}, u32[]{:S(2)}, u32[]{:S(2)}) collective-permute-start(bf16[2,256,768]{2,1,0:T(8,128)(2,1)} %get-tuple-element.18), channel_id=1, source_target_pairs={{6,0},{8,2},{10,4},{12,6},{14,8},{7,1},{9,3},{11,5},{13,7},{15,9},... | collective-permute-start | bytes 2359304 | tf_op jit(solution)/shard_map/ppermute | solution.py:11
  329.6 250.3 %collective-permute-start.7 = (bf16[2,256,768]{2,1,0:T(8,128)(2,1)}, bf16[2,256,768]{2,1,0:T(8,128)(2,1)}, u32[]{:S(2)}, u32[]{:S(2)}) collective-permute-start(bf16[2,256,768]{2,1,0:T(8,128)(2,1)} %get-tuple-element.18), channel_id=1, source_target_pairs={{8,0},{10,2},{12,4},{14,6},{9,1},{11,3},{13,5},{15,7},{24,16},{26,... | collective-permute-start | bytes 2359304 | tf_op jit(solution)/shard_map/ppermute | solution.py:11
  575.6 6.3 copy-start.8
  581.9 195.2 %copy-start.2 = (f32[512,768]{1,0:T(8,128)S(1)}, f32[512,768]{1,0:T(8,128)}, u32[]{:S(2)}) copy-start(f32[512,768]{1,0:T(8,128)} %copy-done.1) | copy-start | bytes 4718596
  581.9 195.2 %copy-start.5 = (bf16[2,256,768]{2,1,0:T(8,128)(2,1)S(1)}, bf16[2,256,768]{2,1,0:T(8,128)(2,1)}, u32[]{:S(2)}) copy-start(bf16[2,256,768]{2,1,0:T(8,128)(2,1)} %param.7) | copy-start | bytes 2359300
  582.0 195.2 %copy-start.10 = (f32[2,256,768]{2,0,1:T(2,128)S(1)}, f32[2,256,768]{2,0,1:T(2,128)}, u32[]{:S(2)}) copy-start(f32[2,256,768]{2,0,1:T(2,128)} %fusion.2) | copy-start | bytes 4718596
  582.0 195.2 %copy-start.13 = (f32[2,256]{1,0:T(2,128)S(1)}, f32[2,256]{1,0:T(2,128)}, u32[]{:S(2)}) copy-start(f32[2,256]{1,0:T(2,128)} %copy-done.11) | copy-start | bytes 6148
  777.2 2.1 copy-start.7
  782.9 245.6 %reduce-scatter.2.cloned.1.call-start = ((), (), s32[]{:S(2)}) async-start(), calls=%async_computation.1 | async-start | bytes 4718592 | tf_op jit(solution)/shard_map/reduce_scatter | solution.py:54
  982.8 4.0 copy-start.3
  (1 other events, 1.2 us)
Sparse Core Ops, SparseCore 0:
  25.2 25.3 all-gather.1
  783.1 199.6 all-reduce.2
  985.0 43.4 reduce-scatter.1
where the time goes:
time: 1050 us; the launch traced here: 1040 us
  matrix products  623 us (59%)
  waiting for transfers between devices  252 us (24%)
  local copies, waits for them, and re-layouts  101 us (10%)
  other arithmetic  27.1 us (3%)
  starting transfers between devices  20.9 us (2%)
  between operations  14.2 us (1%)
    conv_general_dilated x3, matrix products, depthwise(): lax.conv_general_dilated(lhs, kernel[:, None, :], (1,), 'VALID', dimensio...  613 us
    psum x1, waiting for transfers between devices, shards(): filter_sum, proj_sum = lax.psum((filter_local, outer), ('dp', 'seq'))  197 us
    reduce_scatter x1, waiting for transfers between devices, shards(): lax.psum_scatter(partial_out, 'tensor', scatter_dimension=1, tiled=True)  39.1 us
    rev x1, local copies, waits for them, and re-layouts, filter_grad(): return jnp.sum(result.reshape(-1, users, chans), axis=1)[::-1]  24.7 us
    rev x1, local copies, waits for them, and re-layouts, shards(): conv = depthwise(window, filters[::-1])  23 us
  transfers between devices with their start and end apart: 11, of which 4 were waited for; matrix products, arithmetic and copies ran while one was open for 52% of the time, Pallas kernels for 0%

commit v1 on v0

--- a/solution.py
+++ b/solution.py
@@ -72,7 +72,7 @@
     ahead = jnp.concatenate(following, axis=1)[:, : block_len + taps_len - 1]
     grad_input = (depthwise(ahead, filters) * live).astype(jnp.bfloat16)
     filter_local = filter_grad(window, grad_conv)
-    filter_sum, proj_sum = lax.psum((filter_local, outer), ("dp", "seq"))
+    filter_sum, proj_sum = lax.psum(lax.psum((filter_local, outer), "seq"), "dp")
     scale = 1.0 / math.sqrt(users * lax.axis_size("dp") * block_len * lax.axis_size("seq"))
     return (mixed, grad_input, grad_gate, filter_sum * scale, proj_sum * scale)
 

time: 1050 us -> 1250 us (1.19)
  waiting for transfers between devices: 252 us -> 451 us
    psum x1 -> x2, waiting for transfers between devices: 197 us -> 388 us  [the longest x1 201 us: shards(): lax.psum((filter_local, outer), 'seq')]
  transfers between devices with their start and end apart: 11 -> 12, of which waited for: 4 -> 5; matrix products, arithmetic and copies ran while one was open for 52% -> 43% of each run, Pallas kernels for 0% -> 0%
where the time goes in v1:
time: 1250 us; the launch traced here: 1240 us
  matrix products  622 us (50%)
  waiting for transfers between devices  451 us (36%)
  local copies, waits for them, and re-layouts  101 us (8%)
  other arithmetic  27.1 us (2%)
  starting transfers between devices  20.9 us (2%)
  between operations  14.2 us (1%)
    conv_general_dilated x3, matrix products, depthwise(): lax.conv_general_dilated(lhs, kernel[:, None, :], (1,), 'VALID', dimensio...  613 us
    psum x1, waiting for transfers between devices, shards(): lax.psum((filter_local, outer), 'seq')  201 us
    psum x1, waiting for transfers between devices, shards(): lax.psum(lax.psum((filter_local, outer), 'seq'), 'dp')  187 us
    reduce_scatter x1, waiting for transfers between devices, shards(): lax.psum_scatter(partial_out, 'tensor', scatter_dimension=1, tiled=True)  46.4 us
  transfers between devices with their start and end apart: 12, of which 5 were waited for; matrix products, arithmetic and copies ran while one was open for 43% of the time, Pallas kernels for 0%

profile of v1, /device:TPU:0, one launch (start us, length us, event | category | flops | bytes accessed | tf_op | source)
XLA Modules:
  0.0 1236.0 jit_solution(13413072674052777076)
XLA Ops:
  9.5 6.9 collective-permute-start
  16.3 3.6 collective-permute-start.1
  19.9 3.0 collective-permute-start.2
  25.2 23.0 %rev.6 = bf16[1024,768]{1,0:T(8,128)(2,1)} reverse(bf16[1024,768]{1,0:T(8,128)(2,1)} %param.8), dimensions={0} | reverse | bytes 3145728 | tf_op jit(solution)/shard_map/rev | solution.py:47
  51.4 15.7 %collective-permute-done.2 = bf16[2,256,768]{2,1,0:T(8,128)(2,1)} collective-permute-done((bf16[2,256,768]{2,1,0:T(8,128)(2,1)S(1)}, bf16[2,256,768]{2,1,0:T(8,128)(2,1)}, u32[]{:S(2)}, u32[]{:S(2)}) %collective-permute-start.2) | collective-permute-done | bytes 786464 | tf_op jit(solution)/shard_map/ppermute | solution.py:11
  69.7 224.4 %fusion.2 = f32[2,256,768]{2,0,1:T(2,128)} fusion(bf16[2,1280,768]{2,1,0:T(8,128)(2,1)S(1)} %constant_dynamic-update-slice_fusion, bf16[1024,1,768]{2,0,1:T(8,128)(2,1)S(1)} %bitcast.26), kind=kOutput, calls=%fused_computation.3 | convolution fusion | flops 805306368 | bytes 7077888 | tf_op jit(solution)/shard_map/conv_general_dilated | solution.py:15
  294.1 3.0 slice_bitcast_fusion
  297.0 6.2 copy.43
  303.2 16.7 %copy.45 = bf16[1,1279,1536]{2,0,1:T(2,128)(2,1)} copy(bf16[1,1279,1536]{1,2,0:T(8,128)(2,1)} %bitcast.19) | data formatting | bytes 7858176 | tf_op jit(solution)/shard_map/reshape | solution.py:29
  319.9 2.9 fusion.14
  332.2 2.9 copy.46
  335.2 193.4 %convolution_reduce_fusion = f32[1024,1536]{1,0:T(8,128)} fusion(bf16[1,1279,1536]{2,0,1:T(2,128)(2,1)} %copy.45, bf16[256,1,1536]{2,1,0:T(2,128)(2,1)} %copy.46), kind=kOutput, calls=%fused_computation.23 | convolution fusion | flops 805306368 | bytes 11006976 | tf_op jit(solution)/shard_map/conv_general_dilated | solution.py:15
  528.6 8.3 reshape.66
  536.8 11.9 reduce_sum.9
  548.8 24.7 %rev.7 = f32[1024,768]{1,0:T(8,128)} reverse(f32[1024,768]{1,0:T(8,128)} %reduce_sum.9), dimensions={0} | reverse | bytes 6291456 | tf_op jit(solution)/shard_map/rev | solution.py:32
  581.9 195.2 %fusion = f32[2,256,768]{2,0,1:T(2,128)S(1)} fusion(bf16[2,1280,768]{2,1,0:T(8,128)(2,1)} %constant_dynamic-update-slice_fusion.5, bf16[1024,1,768]{2,0,1:T(8,128)(2,1)S(1)} %bitcast.25), kind=kOutput, calls=%fused_computation.1 | convolution fusion | flops 805306368 | bytes 7077888 | tf_op jit(solution)/shard_map/conv_general_dilated | solution.py:15
  779.2 3.6 fusion.15
  782.9 3.1 fusion.13
  786.0 200.5 %all-reduce.5.cloned.1.call-done = (f32[1024,768]{1,0:T(8,128)}, f32[768,1536]{1,0:T(8,128)}) async-done(((f32[1024,768]{1,0:T(8,128)}, f32[768,1536]{1,0:T(8,128)}), (f32[1024,768]{1,0:T(8,128)}, f32[768,1536]{1,0:T(8,128)})) %all-reduce.5.cloned.1.call-update) | async-done | bytes 7864336 | tf_op jit(solution)/shard_map/psum | solution.py:75
  986.6 46.4 %reduce-scatter.2.cloned.1.call-done = f32[512,768]{1,0:T(8,128)} async-done(((f32[512,1536]{1,0:T(8,128)}), f32[512,768]{1,0:T(8,128)}) %reduce-scatter.2.cloned.1.call-update) | async-done | bytes 1572880 | tf_op jit(solution)/shard_map/reduce_scatter | solution.py:54
  1033.0 2.4 convert_element_type.36
  1035.3 187.3 %all-reduce.7.cloned.1.call-done = (f32[1024,768]{1,0:T(8,128)}, f32[768,1536]{1,0:T(8,128)}) async-done(((f32[1024,768]{1,0:T(8,128)}, f32[768,1536]{1,0:T(8,128)}), (f32[1024,768]{1,0:T(8,128)}, f32[768,1536]{1,0:T(8,128)})) %all-reduce.7.cloned.1.call-update) | async-done | bytes 7864336 | tf_op jit(solution)/shard_map/psum | solution.py:75
  1222.6 4.0 broadcast_multiply_fusion.1
  1226.6 2.7 broadcast_multiply_fusion
  (64 shorter events, 30.3 us)
Async XLA Ops:
  7.2 312.8 %copy-start = (bf16[768,1536]{1,0:T(8,128)(2,1)S(1)}, bf16[768,1536]{1,0:T(8,128)(2,1)}, u32[]{:S(2)}) copy-start(bf16[768,1536]{1,0:T(8,128)(2,1)} %param.9) | copy-start | bytes 7077892
  7.2 312.7 %all-gather.2.cloned.1.call-start = ((), (), s32[]{:S(2)}) async-start(), calls=%async_computation.2 | async-start | bytes 2359296 | tf_op jit(solution)/shard_map/all_gather | solution.py:57
  8.1 61.4 %copy-start.11 = (f32[2,256]{1,0:T(2,128)}, f32[2,256]{1,0:T(2,128)S(1)}, u32[]{:S(2)}) copy-start(f32[2,256]{1,0:T(2,128)S(1)} %compare_convert_fusion) | copy-start | bytes 6148
  9.5 38.7 %collective-permute-start = (bf16[2,256,768]{2,1,0:T(8,128)(2,1)S(1)}, bf16[2,256,768]{2,1,0:T(8,128)(2,1)}, u32[]{:S(2)}, u32[]{:S(2)}) collective-permute-start(bf16[2,256,768]{2,1,0:T(8,128)(2,1)S(1)} %multiply_convert_fusion.2), channel_id=1, source_target_pairs={{0,8},{2,10},{4,12},{6,14},{1,9},{3,11},{5,13},{7,15},{16,24},{18,... | collective-permute-start | bytes 2359304 | tf_op jit(solution)/shard_map/ppermute | solution.py:11
  16.3 33.9 %collective-permute-start.1 = (bf16[2,256,768]{2,1,0:T(8,128)(2,1)S(1)}, bf16[2,256,768]{2,1,0:T(8,128)(2,1)}, u32[]{:S(2)}, u32[]{:S(2)}) collective-permute-start(bf16[2,256,768]{2,1,0:T(8,128)(2,1)S(1)} %multiply_convert_fusion.2), channel_id=1, source_target_pairs={{0,6},{2,8},{4,10},{6,12},{8,14},{1,7},{3,9},{5,11},{7,13},{9,15},... | collective-permute-start | bytes 2359304 | tf_op jit(solution)/shard_map/ppermute | solution.py:11
  19.9 47.2 %collective-permute-start.2 = (bf16[2,256,768]{2,1,0:T(8,128)(2,1)S(1)}, bf16[2,256,768]{2,1,0:T(8,128)(2,1)}, u32[]{:S(2)}, u32[]{:S(2)}) collective-permute-start(bf16[2,256,768]{2,1,0:T(8,128)(2,1)S(1)} %multiply_convert_fusion.2), channel_id=1, source_target_pairs={{0,4},{2,6},{4,8},{6,10},{8,12},{10,14},{1,5},{3,7},{5,9},{7,11},{... | collective-permute-start | bytes 2359304 | tf_op jit(solution)/shard_map/ppermute | solution.py:11
  22.9 45.4 %collective-permute-start.3 = (bf16[2,256,768]{2,1,0:T(8,128)(2,1)S(1)}, bf16[2,256,768]{2,1,0:T(8,128)(2,1)}, u32[]{:S(2)}, u32[]{:S(2)}) collective-permute-start(bf16[2,256,768]{2,1,0:T(8,128)(2,1)S(1)} %multiply_convert_fusion.2), channel_id=1, source_target_pairs={{0,2},{2,4},{4,6},{6,8},{8,10},{10,12},{12,14},{1,3},{3,5},{5,7},{... | collective-permute-start | bytes 2359304 | tf_op jit(solution)/shard_map/ppermute | solution.py:11
  25.1 961.5 %all-reduce.5.cloned.1.call-start = ((), (), s32[]{:S(2)}) async-start(), calls=%async_computation.3 | async-start | bytes 15728640 | tf_op jit(solution)/shard_map/psum | solution.py:75
  48.2 21.3 %copy-start.6 = (bf16[2,256,768]{2,1,0:T(8,128)(2,1)S(1)}, bf16[2,256,768]{2,1,0:T(8,128)(2,1)}, u32[]{:S(2)}) copy-start(bf16[2,256,768]{2,1,0:T(8,128)(2,1)} %param.6) | copy-start | bytes 2359300
  49.4 20.3 %copy-start.9 = (bf16[1024,768]{1,0:T(8,128)(2,1)S(1)}, bf16[1024,768]{1,0:T(8,128)(2,1)}, u32[]{:S(2)}) copy-start(bf16[1024,768]{1,0:T(8,128)(2,1)} %rev.6) | copy-start | bytes 4718596
  319.9 4.1 copy-start.4
  319.9 4.1 copy-start.12
  325.6 247.8 %collective-permute-start.4 = (bf16[2,256,768]{2,1,0:T(8,128)(2,1)}, bf16[2,256,768]{2,1,0:T(8,128)(2,1)}, u32[]{:S(2)}, u32[]{:S(2)}) collective-permute-start(bf16[2,256,768]{2,1,0:T(8,128)(2,1)} %get-tuple-element.20), channel_id=1, source_target_pairs={{2,0},{4,2},{6,4},{8,6},{10,8},{12,10},{14,12},{3,1},{5,3},{7,5},{... | collective-permute-start | bytes 2359304 | tf_op jit(solution)/shard_map/ppermute | solution.py:11
  326.9 248.7 %collective-permute-start.5 = (bf16[2,256,768]{2,1,0:T(8,128)(2,1)}, bf16[2,256,768]{2,1,0:T(8,128)(2,1)}, u32[]{:S(2)}, u32[]{:S(2)}) collective-permute-start(bf16[2,256,768]{2,1,0:T(8,128)(2,1)} %get-tuple-element.20), channel_id=1, source_target_pairs={{4,0},{6,2},{8,4},{10,6},{12,8},{14,10},{5,1},{7,3},{9,5},{11,7},{... | collective-permute-start | bytes 2359304 | tf_op jit(solution)/shard_map/ppermute | solution.py:11
  328.2 249.5 %collective-permute-start.6 = (bf16[2,256,768]{2,1,0:T(8,128)(2,1)}, bf16[2,256,768]{2,1,0:T(8,128)(2,1)}, u32[]{:S(2)}, u32[]{:S(2)}) collective-permute-start(bf16[2,256,768]{2,1,0:T(8,128)(2,1)} %get-tuple-element.20), channel_id=1, source_target_pairs={{6,0},{8,2},{10,4},{12,6},{14,8},{7,1},{9,3},{11,5},{13,7},{15,9},... | collective-permute-start | bytes 2359304 | tf_op jit(solution)/shard_map/ppermute | solution.py:11
  329.5 250.3 %collective-permute-start.7 = (bf16[2,256,768]{2,1,0:T(8,128)(2,1)}, bf16[2,256,768]{2,1,0:T(8,128)(2,1)}, u32[]{:S(2)}, u32[]{:S(2)}) collective-permute-start(bf16[2,256,768]{2,1,0:T(8,128)(2,1)} %get-tuple-element.20), channel_id=1, source_target_pairs={{8,0},{10,2},{12,4},{14,6},{9,1},{11,3},{13,5},{15,7},{24,16},{26,... | collective-permute-start | bytes 2359304 | tf_op jit(solution)/shard_map/ppermute | solution.py:11
  573.5 8.4 copy-start.8
  581.9 195.2 %copy-start.2 = (f32[512,768]{1,0:T(8,128)S(1)}, f32[512,768]{1,0:T(8,128)}, u32[]{:S(2)}) copy-start(f32[512,768]{1,0:T(8,128)} %copy-done.1) | copy-start | bytes 4718596
  581.9 195.2 %copy-start.5 = (bf16[2,256,768]{2,1,0:T(8,128)(2,1)S(1)}, bf16[2,256,768]{2,1,0:T(8,128)(2,1)}, u32[]{:S(2)}) copy-start(bf16[2,256,768]{2,1,0:T(8,128)(2,1)} %param.7) | copy-start | bytes 2359300
  581.9 195.2 %copy-start.10 = (f32[2,256,768]{2,0,1:T(2,128)S(1)}, f32[2,256,768]{2,0,1:T(2,128)}, u32[]{:S(2)}) copy-start(f32[2,256,768]{2,0,1:T(2,128)} %fusion.2) | copy-start | bytes 4718596
  581.9 195.2 %copy-start.13 = (f32[2,256]{1,0:T(2,128)S(1)}, f32[2,256]{1,0:T(2,128)}, u32[]{:S(2)}) copy-start(f32[2,256]{1,0:T(2,128)} %copy-done.11) | copy-start | bytes 6148
  782.9 250.1 %reduce-scatter.2.cloned.1.call-start = ((), (), s32[]{:S(2)}) async-start(), calls=%async_computation.1 | async-start | bytes 4718592 | tf_op jit(solution)/shard_map/reduce_scatter | solution.py:54
  786.0 436.6 %all-reduce.7.cloned.1.call-start = ((), (), s32[]{:S(2)}) async-start(), calls=%async_computation.4 | async-start | bytes 15728640 | tf_op jit(solution)/shard_map/psum | solution.py:75
  1222.6 4.0 copy-start.3
  (2 other events, 3.3 us)
Sparse Core Ops, SparseCore 0:
  25.2 25.3 all-gather.1
  783.0 203.5 all-reduce.4
  989.4 43.5 reduce-scatter.1
  1035.3 187.2 all-reduce.6
